TPU v7x, 256 devices: a whole 4x4x8 slice. The times are simulated.
256 devices in a mesh: leaf: 16 (over y, x), row: 16 (over z, core).
Axes of the slice: x: 4, y: 4, z: 8, core: 2. Of those that a mesh axis runs over, the one named last changes fastest.
Arguments:
- sigma_root: float32 [2048, 2048], P(None, 'row')
- linv_one: bfloat16 [16, 2048, 2048], P('leaf', None, 'row'), as said below
- panel_one: bfloat16 [16, 512, 2048], P('leaf', None, 'row'), may hold values from -1.25 to 1.25
- tiles_one: int32 [16, 4], replicated, may hold values from 0 to 15, as said below
- mask_one: int32 [16, 4, 16], P('leaf', None, 'row'), may hold values 0 or 1
- linv_two: bfloat16 [16, 2048, 2048], P('leaf', None, 'row'), as said below
- panel_two: bfloat16 [16, 512, 2048], P('leaf', None, 'row'), may hold values from -1.25 to 1.25
- tiles_two: int32 [16, 4], replicated, may hold values from 0 to 15, as said below
- mask_two: int32 [16, 4, 16], P('leaf', None, 'row'), may hold values 0 or 1
- parent: int32 [16], replicated, may hold values from 0 to 15
Outputs:
- sigma_one: float32 [16, 2048, 2048], P('leaf', None, 'row')
- cross_one: float32 [16, 512, 2048], P('leaf', None, 'row')
- sigma_two: float32 [16, 2048, 2048], P('leaf', None, 'row')
- cross_two: float32 [16, 512, 2048], P('leaf', None, 'row')
Inputs may be any that keep to these rules, and one draw needn't show every extreme that they name: `tiles_one`: each row holds 4 different tile numbers in increasing order. `tiles_two`: each row holds 4 different tile numbers in increasing order. `linv_one`: each block is lower triangular with a positive diagonal. `sigma_root`: symmetric. `linv_two`: each block is lower triangular with a positive diagonal.
All inputs are finite; a program needn't handle non-finite values. No bound on the sum of `mask_one` or of `mask_two` on one device may be relied on, other than what follows from the above.
Results may differ from a plain program's by a relative error of at most 0.00045.
Values may be sent and summed in bfloat16 or wider, within the bound.
No kernel may reach another device: no remote copies, remote signals or barrier semaphores. Data moves between devices by JAX's collectives and lax.ppermute only.
A program may use at most 64 MiB of HBM per device.

v0:
```python
import jax
import jax.numpy as jnp
from jax import lax
from jax.sharding import PartitionSpec as P

TILE = 128


def pattern_rows(tile_list):
    offsets = jnp.arange(TILE, dtype=jnp.int32)
    return (tile_list[..., None] * TILE + offsets).reshape(tile_list.shape[:-1] + (-1,))


def expand_mask(tile_mask):
    return jnp.repeat(jnp.repeat(tile_mask, TILE, axis=0), TILE, axis=1)


def assemble(selected, row_list):
    gathered = lax.all_gather(selected, "row", axis=1, tiled=True)
    return jnp.take(gathered, row_list, axis=1)


def solve_block(selected, row_list, linv_local, panel_local, mask_local):
    select = assemble(selected, row_list)
    masked = panel_local * expand_mask(mask_local).astype(jnp.bfloat16)
    linv_wide = linv_local.astype(jnp.float32)
    whole_panel = lax.all_gather(masked, "row", axis=1, tiled=True)
    upper_part = jnp.dot(whole_panel, linv_local, preferred_element_type=jnp.float32)
    cross = -jnp.dot(select, upper_part, precision=lax.Precision.HIGHEST)
    middle = linv_wide - jnp.dot(
        whole_panel.astype(jnp.float32).T, cross, precision=lax.Precision.HIGHEST
    )
    sigma = jnp.dot(
        lax.all_gather(linv_local, "row", axis=1, tiled=True).astype(jnp.float32).T,
        middle,
        precision=lax.Precision.HIGHEST,
    )
    return (sigma, cross)


def body(
    sigma_root,
    linv_one,
    panel_one,
    tiles_one,
    mask_one,
    linv_two,
    panel_two,
    tiles_two,
    mask_two,
    parent,
):
    leaf_id = lax.axis_index("leaf")
    width = sigma_root.shape[1]
    own_tiles = lax.dynamic_index_in_dim(tiles_one, leaf_id, 0, keepdims=False)
    rows_first = pattern_rows(own_tiles)
    selected_first = jnp.take(sigma_root, rows_first, axis=0)
    sigma_first, cross_first = solve_block(
        selected_first, rows_first, linv_one[0], panel_one[0], mask_one[0]
    )
    rows_every = pattern_rows(tiles_two)
    count = rows_every.shape[0]
    block_rows = rows_every.shape[1]
    owned = (parent == leaf_id).astype(jnp.float32)
    slots = jnp.take(sigma_first, rows_every.reshape(-1), axis=0).reshape(count, block_rows, width)
    slots = slots * owned[:, None, None]
    arrived = lax.all_to_all(slots, "leaf", split_axis=0, concat_axis=0, tiled=True)
    selected_second = jnp.sum(arrived, axis=0)
    rows_second = lax.dynamic_index_in_dim(rows_every, leaf_id, 0, keepdims=False)
    sigma_second, cross_second = solve_block(
        selected_second, rows_second, linv_two[0], panel_two[0], mask_two[0]
    )
    return (sigma_first[None], cross_first[None], sigma_second[None], cross_second[None])


def solution(mesh):
    return jax.shard_map(
        body,
        mesh=mesh,
        in_specs=(
            P(None, "row"),
            P("leaf", None, "row"),
            P("leaf", None, "row"),
            P(),
            P("leaf", None, "row"),
            P("leaf", None, "row"),
            P("leaf", None, "row"),
            P(),
            P("leaf", None, "row"),
            P(),
        ),
        out_specs=(
            P("leaf", None, "row"),
            P("leaf", None, "row"),
            P("leaf", None, "row"),
            P("leaf", None, "row"),
        ),
        check_vma=False,
    )
```

profile of v0, /device:TPU:1, one launch (start us, length us, event | category | flops | bytes accessed | tf_op | source)
XLA Modules:
  0.0 404.3 jit_solution(16791441184361963141)
XLA Ops:
  7.2 0.8 convert_bitcast_fusion.1
  8.0 0.1 broadcast_bitcast_fusion.1
  8.1 1.7 bitcast_multiply_fusion.1
  9.9 0.9 multiply_reduce_fusion
  10.7 0.1 iota_add_fusion.1
  10.8 1.0 gather_fusion
  11.9 0.1 compare_and_fusion.2
  11.9 0.8 broadcast_select_fusion
  12.8 0.0 all-gather.17.cloned.1.call-start
  12.9 0.7 all-gather.17.cloned.1.call-update
  13.5 0.7 broadcast_multiply_fusion
  14.2 0.1 copy.20
  14.3 0.1 compare_select_fusion.4
  14.4 0.7 compare_convert_fusion
  15.1 0.7 convert_bitcast_fusion
  15.7 0.1 broadcast_bitcast_fusion
  15.8 0.1 iota_add_fusion
  15.9 0.1 add.146
  16.1 39.5 %all-gather.9.cloned.1.call-done = bf16[512,2048]{1,0:T(8,128)(2,1)} async-done(((bf16[512,128]{1,0:T(8,128)(2,1)}), bf16[512,2048]{1,0:T(8,128)(2,1)}) %all-gather.9.cloned.1.call-update) | async-done | bytes 2097168 | tf_op jit(solution)/shard_map/all_gather | solution.py:27
  55.5 2.3 fusion.13
  57.8 48.6 %all-gather.11.cloned.1.call-done = f32[512,2048]{1,0:T(8,128)} async-done(((f32[512,128]{1,0:T(8,128)}), f32[512,2048]{1,0:T(8,128)}) %all-gather.11.cloned.1.call-update) | async-done | bytes 4194320 | tf_op jit(solution)/shard_map/all_gather | solution.py:19
  106.5 5.3 %copy.19 = f32[512,2048]{0,1:T(8,128)} copy(f32[512,2048]{1,0:T(8,128)} %all-gather.11.cloned.1.call-done) | data formatting | bytes 8388608 | tf_op jit(solution)/shard_map/all_gather | solution.py:19
  111.8 4.2 %gather_fusion.2 = f32[512,512]{1,0:T(8,128)S(1)} fusion(f32[512,2048]{0,1:T(8,128)} %copy.19, s32[1024]{0:T(1024)S(1)} %pad_clamp_fusion.1), kind=kCustom, calls=%fused_computation.clone | custom fusion | bytes 2099200 | tf_op jit(solution)/shard_map/jit(_take)/gather | solution.py:20
  116.0 1.9 convolution_negate_fusion.1
  117.9 0.7 copy-done.4
  118.6 3.9 convolution_subtract_fusion.1
  122.6 50.3 %all-gather.17.cloned.1.call-done = bf16[1,2048,2048]{2,1,0:T(8,128)(2,1)} async-done(((bf16[1,2048,128]{2,1,0:T(8,128)(2,1)}), bf16[1,2048,2048]{2,1,0:T(8,128)(2,1)}) %all-gather.17.cloned.1.call-update) | async-done | bytes 8388624 | tf_op jit(solution)/shard_map/all_gather | solution.py:34
  172.9 6.3 %fusion.2 = f32[128,2048]{1,0:T(8,128)S(1)} fusion(f32[2048,128]{1,0:T(8,128)S(1)} %convolution_subtract_fusion.1, bf16[1,2048,2048]{2,1,0:T(8,128)(2,1)} %all-gather.17.cloned.1.call-done), kind=kOutput, calls=%fused_computation.6 | convolution fusion | flops 6442450944 | bytes 10485760 | tf_op jit(solution)/shard_map/dot_general | solution.py:33
  179.1 0.3 copy.21
  179.5 27.8 %gather_fusion.1 = f32[8192,128]{1,0:T(8,128)} fusion(f32[2048,128]{1,0:T(8,128)S(1)} %copy.21, s32[8192]{0:T(1024)S(1)} %broadcast_clamp_fusion), kind=kCustom, calls=%fused_computation.3 | custom fusion | bytes 8421376 | tf_op jit(solution)/shard_map/jit(_take)/gather | solution.py:65
  207.3 5.3 %select_multiply_fusion = f32[16,512,128]{2,1,0:T(8,128)} fusion(f32[16,512,128]{2,1,0:T(8,128)} %bitcast.84, f32[16]{0:T(128)S(1)} %compare_convert_fusion, pred[16,512]{1,0:T(8,128)(4,1)S(1)} %compare_and_fusion), kind=kLoop, calls=%fused_computation.8 | loop fusion | flops 2097152 | bytes 8396864 | tf_op jit(solution)/shard_map/mul | solution.py:66
  212.5 4.7 %all-to-all-start = ((f32[16,512,128]{2,1,0:T(8,128)}), f32[16,512,128]{2,1,0:T(8,128)}, u32[]{:S(2)}, u32[]{:S(2)}) async-start(f32[16,512,128]{2,1,0:T(8,128)} %select_multiply_fusion), calls=%async_computation | async-start | bytes 8388608 | tf_op jit(solution)/shard_map/all_to_all | solution.py:67
  217.3 0.8 bitcast_multiply_fusion
  218.1 0.0 all-gather.15.cloned.1.call-start
  218.2 62.3 %all-to-all-done = f32[16,512,128]{2,1,0:T(8,128)} async-done(((f32[16,512,128]{2,1,0:T(8,128)}), f32[16,512,128]{2,1,0:T(8,128)}, u32[]{:S(2)}, u32[]{:S(2)}) %all-to-all-start) | async-done | bytes 4194336 | tf_op jit(solution)/shard_map/all_to_all | solution.py:67
  280.5 2.4 reduce_sum.9
  282.9 0.8 copy.22
  283.7 0.2 all-gather.19.cloned.1.call-start
  284.0 0.3 all-gather.19.cloned.1.call-update
  284.4 2.3 fusion.11
  286.7 1.3 copy.23
  288.0 35.5 %all-gather.15.cloned.1.call-done = f32[512,2048]{0,1:T(8,128)} async-done(((f32[512,128]{0,1:T(8,128)}), f32[512,2048]{0,1:T(8,128)}) %all-gather.15.cloned.1.call-update) | async-done | bytes 4194320 | tf_op jit(solution)/shard_map/all_gather | solution.py:19
  323.6 4.2 %gather_fusion.3 = f32[512,512]{1,0:T(8,128)S(1)} fusion(f32[512,2048]{0,1:T(8,128)} %all-gather.15.cloned.1.call-done, s32[1024]{0:T(1024)S(1)} %pad_clamp_fusion), kind=kCustom, calls=%fused_computation.1.clone | custom fusion | bytes 2099200 | tf_op jit(solution)/shard_map/jit(_take)/gather | solution.py:20
  327.8 1.9 convolution_negate_fusion
  329.7 4.0 convolution_subtract_fusion
  333.7 56.2 %all-gather.19.cloned.1.call-done = bf16[1,2048,2048]{2,1,0:T(8,128)(2,1)} async-done(((bf16[1,2048,128]{2,1,0:T(8,128)(2,1)}), bf16[1,2048,2048]{2,1,0:T(8,128)(2,1)}) %all-gather.19.cloned.1.call-update) | async-done | bytes 8388624 | tf_op jit(solution)/shard_map/all_gather | solution.py:34
  389.9 6.3 %fusion.4 = f32[1,2048,128]{1,2,0:T(8,128)S(1)} fusion(f32[2048,128]{1,0:T(8,128)S(1)} %convolution_subtract_fusion, bf16[1,2048,2048]{2,1,0:T(8,128)(2,1)} %all-gather.19.cloned.1.call-done), kind=kOutput, calls=%fused_computation.9 | convolution fusion | flops 6442450944 | bytes 10485760 | tf_op jit(solution)/shard_map/dot_general | solution.py:33
  396.2 1.3 copy.24
  (34 shorter events, 0.4 us)
Async XLA Ops:
  7.2 3.6 copy-start
  7.2 48.4 %copy-start.1 = (bf16[1,2048,128]{2,1,0:T(8,128)(2,1)S(1)}, bf16[1,2048,128]{2,1,0:T(8,128)(2,1)}, u32[]{:S(2)}) copy-start(bf16[1,2048,128]{2,1,0:T(8,128)(2,1)} %param.13) | copy-start | bytes 1572868
  7.2 48.3 %all-gather.9.cloned.1.call-start = ((), (), s32[]{:S(2)}) async-start(), calls=%async_computation.1 | async-start | bytes 2228224 | tf_op jit(solution)/shard_map/all_gather | solution.py:27
  9.8 96.7 %all-gather.11.cloned.1.call-start = ((), (), s32[]{:S(2)}) async-start(), calls=%async_computation.2 | async-start | bytes 4456448 | tf_op jit(solution)/shard_map/all_gather | solution.py:19
  12.8 160.1 %all-gather.17.cloned.1.call-start = ((), (), s32[]{:S(2)}) async-start(), calls=%async_computation.5 | async-start | bytes 8912896 | tf_op jit(solution)/shard_map/all_gather | solution.py:34
  117.9 0.7 copy-start.4
  212.5 4.8 %copy-start.6 = (bf16[1,512,128]{2,1,0:T(8,128)(2,1)S(1)}, bf16[1,512,128]{2,1,0:T(8,128)(2,1)}, u32[]{:S(2)}) copy-start(bf16[1,512,128]{2,1,0:T(8,128)(2,1)} %param.18) | copy-start | bytes 393220
  212.5 67.9 %all-to-all-start = ((f32[16,512,128]{2,1,0:T(8,128)}), f32[16,512,128]{2,1,0:T(8,128)}, u32[]{:S(2)}, u32[]{:S(2)}) async-start(f32[16,512,128]{2,1,0:T(8,128)} %select_multiply_fusion), calls=%async_computation | async-start | bytes 8388608 | tf_op jit(solution)/shard_map/all_to_all | solution.py:67
  217.2 67.2 %copy-start.2 = (bf16[1,2048,128]{2,1,0:T(8,128)(2,1)S(1)}, bf16[1,2048,128]{2,1,0:T(8,128)(2,1)}, u32[]{:S(2)}) copy-start(bf16[1,2048,128]{2,1,0:T(8,128)(2,1)} %param.17) | copy-start | bytes 1572868
  217.2 67.2 %all-gather.13.cloned.1.call-start = ((), (), s32[]{:S(2)}) async-start(), calls=%async_computation.3 | async-start | bytes 2228224 | tf_op jit(solution)/shard_map/all_gather | solution.py:27
  218.1 105.4 %all-gather.15.cloned.1.call-start = ((), (), s32[]{:S(2)}) async-start(), calls=%async_computation.4 | async-start | bytes 4456448 | tf_op jit(solution)/shard_map/all_gather | solution.py:19
  283.7 106.2 %all-gather.19.cloned.1.call-start = ((), (), s32[]{:S(2)}) async-start(), calls=%async_computation.6 | async-start | bytes 8912896 | tf_op jit(solution)/shard_map/all_gather | solution.py:34
  288.0 41.6 %copy-start.3 = (bf16[1,2048,128]{2,1,0:T(8,128)(2,1)S(1)}, bf16[1,2048,128]{2,1,0:T(8,128)(2,1)}, u32[]{:S(2)}) copy-start(bf16[1,2048,128]{2,1,0:T(8,128)(2,1)} %param.17) | copy-start | bytes 1572868
  329.7 4.0 copy-start.5
Sparse Core Ops, SparseCore 0:
  10.4 45.1 all-gather.8
  57.9 48.5 all-gather.10
  108.2 64.6 all-gather.16
  220.1 40.0 all-gather.12
  283.9 39.6 all-gather.14
  325.2 64.6 all-gather.18
where the time goes:
time: 405 us; the launch traced here: 404 us
  waiting for transfers between devices  294 us (73%)
  local copies, waits for them, and re-layouts  47.4 us (12%)
  matrix products  28.8 us (7%)
  other arithmetic  15.1 us (4%)
  between operations  14.4 us (4%)
  starting transfers between devices  5.12 us (1%)
    all_gather x2, waiting for transfers between devices, solve_block(): lax.all_gather(linv_local, 'row', axis=1, tiled=True).astype(jnp.float32)  107 us
    all_gather x2, waiting for transfers between devices, assemble(): gathered = lax.all_gather(selected, 'row', axis=1, tiled=True)  84.1 us
    all_to_all x1, waiting for transfers between devices, body(): lax.all_to_all(slots, 'leaf', split_axis=0, concat_axis=0, tiled=True)  62.3 us
    all_gather x2, waiting for transfers between devices, solve_block(): whole_panel = lax.all_gather(masked, 'row', axis=1, tiled=True)  39.5 us
    gather x1, local copies, waits for them, and re-layouts, body(): jnp.take(sigma_first, rows_every.reshape(-1), axis=0)  27.8 us
    dot_general x2, matrix products, solve_block(): jnp.dot(lax.all_gather(linv_local, 'row', axis=1, tiled=True).astype(jnp....  12.5 us
    gather x2, local copies, waits for them, and re-layouts, assemble(): return jnp.take(gathered, row_list, axis=1)  8.43 us
  transfers between devices with their start and end apart: 7, of which 6 were waited for; matrix products, arithmetic and copies ran while one was open for 10% of the time, Pallas kernels for 0%

commit v1 on v0

--- a/solution.py
+++ b/solution.py
@@ -16,7 +16,22 @@
 
 
 def assemble(selected, row_list):
-    gathered = lax.all_gather(selected, "row", axis=1, tiled=True)
+    length, mine, span = (lax.axis_size("row"), lax.axis_index("row"), selected.shape[1])
+    forward = [(i, (i + 1) % length) for i in range(length)]
+    downward = [(i, (i - 1) % length) for i in range(length)]
+    out = jnp.zeros((*selected.shape[:1], length * span, *selected.shape[1 + 1 :]), selected.dtype)
+    out = lax.dynamic_update_slice_in_dim(out, selected, mine * span, axis=1)
+    from_left = from_right = selected
+    halfway = length // 2
+    for step in range(1, halfway + 1):
+        from_left = lax.ppermute(from_left, "row", forward)
+        out = lax.dynamic_update_slice_in_dim(out, from_left, (mine - step) % length * span, axis=1)
+        if step < length - halfway:
+            from_right = lax.ppermute(from_right, "row", downward)
+            out = lax.dynamic_update_slice_in_dim(
+                out, from_right, (mine + step) % length * span, axis=1
+            )
+    gathered = out
     return jnp.take(gathered, row_list, axis=1)
 
 

time: 405 us -> 319 us (0.79)
  waiting for transfers between devices: 294 us -> 120 us
  starting transfers between devices: 5.12 us -> 68.7 us
  local copies, waits for them, and re-layouts: 47.4 us -> 71.1 us
    all_gather x2 -> x0, waiting for transfers between devices: 84.1 us -> none  [assemble(): gathered = lax.all_gather(selected, 'row', axis=1, tiled=True)]
    all_gather x2, waiting for transfers between devices: 107 us -> 39 us  [solve_block(): lax.all_gather(linv_local, 'row', axis=1, tiled=True).astype(jnp.float32)]
    ppermute x0 -> x30, starting transfers between devices: none -> 61.6 us  [the longest x14 46.8 us: assemble(): from_right = lax.ppermute(from_right, 'row', downward)]
    all_gather x2, waiting for transfers between devices: 39.5 us -> 0.02 us  [solve_block(): whole_panel = lax.all_gather(masked, 'row', axis=1, tiled=True)]
    dynamic_update_slice x0 -> x32, local copies, waits for them, and re-layouts: none -> 23.2 us  [the longest x16 11.5 us: assemble(): lax.dynamic_update_slice_in_dim(out, from_left, (mine - step) % length *...]
    ppermute x0 -> x30, waiting for transfers between devices: none -> 16.4 us  [the longest x16 14.8 us: assemble(): from_left = lax.ppermute(from_left, 'row', forward)]
    all_gather x1 -> x0, local copies, waits for them, and re-layouts: 5.34 us -> none  [assemble(): gathered = lax.all_gather(selected, 'row', axis=1, tiled=True)]
    another operation x0 -> x2, local copies, waits for them, and re-layouts: none -> 5.08 us
  transfers between devices with their start and end apart: 7 -> 35, of which waited for: 6 -> 12; matrix products, arithmetic and copies ran while one was open for 10% -> 32% of each run, Pallas kernels for 0% -> 0%
where the time goes in v1:
time: 319 us; the launch traced here: 315 us
  waiting for transfers between devices  120 us (38%)
  local copies, waits for them, and re-layouts  71.1 us (22%)
  starting transfers between devices  68.7 us (22%)
  matrix products  27.4 us (9%)
  between operations  14.6 us (5%)
  other arithmetic  13.9 us (4%)
    all_to_all x1, waiting for transfers between devices, body(): lax.all_to_all(slots, 'leaf', split_axis=0, concat_axis=0, tiled=True)  62.9 us
    ppermute x14, starting transfers between devices, assemble(): from_right = lax.ppermute(from_right, 'row', downward)  46.8 us
    all_gather x2, waiting for transfers between devices, solve_block(): lax.all_gather(linv_local, 'row', axis=1, tiled=True).astype(jnp.float32)  39 us
    gather x1, local copies, waits for them, and re-layouts, body(): jnp.take(sigma_first, rows_every.reshape(-1), axis=0)  27.7 us
    ppermute x16, waiting for transfers between devices, assemble(): from_left = lax.ppermute(from_left, 'row', forward)  14.8 us
    ppermute x16, starting transfers between devices, assemble(): from_left = lax.ppermute(from_left, 'row', forward)  14.8 us
    dot_general x2, matrix products, solve_block(): jnp.dot(lax.all_gather(linv_local, 'row', axis=1, tiled=True).astype(jnp....  12.6 us
    dynamic_update_slice x16, local copies, waits for them, and re-layouts, assemble(): lax.dynamic_update_slice_in_dim(out, from_left, (mine - step) % length *...  11.5 us
  transfers between devices with their start and end apart: 35, of which 12 were waited for; matrix products, arithmetic and copies ran while one was open for 32% of the time, Pallas kernels for 0%

profile of v1, /device:TPU:1, one launch (start us, length us, event | category | flops | bytes accessed | tf_op | source)
XLA Modules:
  0.0 315.2 jit_solution(15474487919823765811)
XLA Ops:
  8.1 1.7 bitcast_multiply_fusion.1
  11.3 1.7 bitcast_multiply_fusion
  13.6 0.9 fusion.20
  14.6 1.0 gather_fusion
  15.8 3.0 collective-permute-start
  19.4 2.8 collective-permute-done
  22.2 2.5 collective-permute-start.2
  25.0 2.8 collective-permute-start.3
  27.9 1.5 collective-permute-done.2
  29.4 2.5 collective-permute-start.4
  31.9 4.8 %collective-permute-start.5 = (f32[512,128]{1,0:T(8,128)S(1)}, f32[512,128]{1,0:T(8,128)S(1)}, u32[]{:S(2)}, u32[]{:S(2)}) collective-permute-start(f32[512,128]{1,0:T(8,128)S(1)} %collective-permute-done.3), channel_id=1, source_target_pairs={{0,15},{1,0},{2,1},{3,2},{4,3},{5,4},{6,5},{7,6},{8,7},{9,8},{10,9... | collective-permute-start | bytes 786440 | tf_op jit(solution)/shard_map/ppermute | solution.py:30
  36.9 2.5 broadcast.110.clone
  40.5 4.4 %collective-permute-start.7 = (f32[512,128]{1,0:T(8,128)S(1)}, f32[512,128]{1,0:T(8,128)S(1)}, u32[]{:S(2)}, u32[]{:S(2)}) collective-permute-start(f32[512,128]{1,0:T(8,128)S(1)} %collective-permute-done.5), channel_id=1, source_target_pairs={{0,15},{1,0},{2,1},{3,2},{4,3},{5,4},{6,5},{7,6},{8,7},{9,8},{10,9... | collective-permute-start | bytes 786440 | tf_op jit(solution)/shard_map/ppermute | solution.py:30
  48.0 5.3 %collective-permute-start.9 = (f32[512,128]{1,0:T(8,128)S(1)}, f32[512,128]{1,0:T(8,128)S(1)}, u32[]{:S(2)}, u32[]{:S(2)}) collective-permute-start(f32[512,128]{1,0:T(8,128)S(1)} %collective-permute-done.7), channel_id=1, source_target_pairs={{0,15},{1,0},{2,1},{3,2},{4,3},{5,4},{6,5},{7,6},{8,7},{9,8},{10,9... | collective-permute-start | bytes 786440 | tf_op jit(solution)/shard_map/ppermute | solution.py:30
  55.9 4.4 %collective-permute-start.11 = (f32[512,128]{1,0:T(8,128)S(1)}, f32[512,128]{1,0:T(8,128)S(1)}, u32[]{:S(2)}, u32[]{:S(2)}) collective-permute-start(f32[512,128]{1,0:T(8,128)S(1)} %collective-permute-done.9), channel_id=1, source_target_pairs={{0,15},{1,0},{2,1},{3,2},{4,3},{5,4},{6,5},{7,6},{8,7},{9,8},{10,9... | collective-permute-start | bytes 786440 | tf_op jit(solution)/shard_map/ppermute | solution.py:30
  62.9 4.4 %collective-permute-start.13 = (f32[512,128]{1,0:T(8,128)S(1)}, f32[512,128]{1,0:T(8,128)S(1)}, u32[]{:S(2)}, u32[]{:S(2)}) collective-permute-start(f32[512,128]{1,0:T(8,128)S(1)} %collective-permute-done.11), channel_id=1, source_target_pairs={{0,15},{1,0},{2,1},{3,2},{4,3},{5,4},{6,5},{7,6},{8,7},{9,8},{10,9... | collective-permute-start | bytes 786440 | tf_op jit(solution)/shard_map/ppermute | solution.py:30
  71.5 3.5 %collective-permute-done.14 = f32[512,128]{1,0:T(8,128)S(1)} collective-permute-done((f32[512,128]{1,0:T(8,128)S(1)}, f32[512,128]{1,0:T(8,128)S(1)}, u32[]{:S(2)}, u32[]{:S(2)}) %collective-permute-start.14) | collective-permute-done | bytes 262176 | tf_op jit(solution)/shard_map/ppermute | solution.py:27
  75.9 4.3 %gather_fusion.2 = f32[512,512]{1,0:T(8,128)S(1)} fusion(f32[512,2048]{0,1:T(8,128)} %constant_dynamic-update-slice_fusion.16, s32[1024]{0:T(1024)S(1)} %pad_clamp_fusion.1), kind=kCustom, calls=%fused_computation.clone | custom fusion | bytes 2099200 | tf_op jit(solution)/shard_map/jit(_take)/gather | solution.py:35
  80.2 2.5 fusion.13
  82.6 1.9 convolution_negate_fusion.1
  84.6 2.3 convolution_subtract_fusion.1
  86.9 39.0 %all-gather.11.cloned.1.call-done = bf16[1,2048,2048]{2,1,0:T(8,128)(2,1)} async-done(((bf16[1,2048,128]{2,1,0:T(8,128)(2,1)}), bf16[1,2048,2048]{2,1,0:T(8,128)(2,1)}) %all-gather.11.cloned.1.call-update) | async-done | bytes 8388624 | tf_op jit(solution)/shard_map/all_gather | solution.py:49
  125.9 6.3 %fusion.2 = f32[128,2048]{1,0:T(8,128)S(1)} fusion(f32[2048,128]{1,0:T(8,128)S(1)} %convolution_subtract_fusion.1, bf16[1,2048,2048]{2,1,0:T(8,128)(2,1)} %all-gather.11.cloned.1.call-done), kind=kOutput, calls=%fused_computation.6 | convolution fusion | flops 6442450944 | bytes 10485760 | tf_op jit(solution)/shard_map/dot_general | solution.py:48
  132.5 27.7 %gather_fusion.1 = f32[8192,128]{1,0:T(8,128)} fusion(f32[2048,128]{1,0:T(8,128)S(1)} %copy.51, s32[8192]{0:T(1024)S(1)} %broadcast_clamp_fusion), kind=kCustom, calls=%fused_computation.3 | custom fusion | bytes 8421376 | tf_op jit(solution)/shard_map/jit(_take)/gather | solution.py:80
  160.2 5.3 %select_multiply_fusion = f32[16,512,128]{2,1,0:T(8,128)} fusion(f32[16,512,128]{2,1,0:T(8,128)} %bitcast.84, f32[16]{0:T(128)S(1)} %compare_convert_fusion, pred[16,512]{1,0:T(8,128)(4,1)S(1)} %compare_and_fusion), kind=kLoop, calls=%fused_computation.8 | loop fusion | flops 2097152 | bytes 8396864 | tf_op jit(solution)/shard_map/mul | solution.py:81
  165.5 6.9 %all-to-all-start = ((f32[16,512,128]{2,1,0:T(8,128)}), f32[16,512,128]{2,1,0:T(8,128)}, u32[]{:S(2)}, u32[]{:S(2)}) async-start(f32[16,512,128]{2,1,0:T(8,128)} %select_multiply_fusion), calls=%async_computation | async-start | bytes 8388608 | tf_op jit(solution)/shard_map/all_to_all | solution.py:82
  172.5 62.9 %all-to-all-done = f32[16,512,128]{2,1,0:T(8,128)} async-done(((f32[16,512,128]{2,1,0:T(8,128)}), f32[16,512,128]{2,1,0:T(8,128)}, u32[]{:S(2)}, u32[]{:S(2)}) %all-to-all-start) | async-done | bytes 4194336 | tf_op jit(solution)/shard_map/all_to_all | solution.py:82
  235.4 2.4 reduce_sum.9
  237.9 1.2 collective-permute-start.15
  239.3 3.1 collective-permute-done.15
  242.5 2.5 collective-permute-start.17
  245.2 1.1 collective-permute-start.18
  246.3 1.9 collective-permute-done.17
  248.3 2.5 collective-permute-start.19
  251.3 2.0 collective-permute-start.20
  253.3 2.3 fusion.11
  255.6 1.3 copy.55
  257.0 2.6 broadcast.110
  261.0 3.4 %collective-permute-start.22 = (f32[512,128]{0,1:T(8,128)S(1)}, f32[512,128]{0,1:T(8,128)S(1)}, u32[]{:S(2)}, u32[]{:S(2)}) collective-permute-start(f32[512,128]{0,1:T(8,128)S(1)} %collective-permute-done.20), channel_id=1, source_target_pairs={{0,15},{1,0},{2,1},{3,2},{4,3},{5,4},{6,5},{7,6},{8,7},{9,8},{10,9... | collective-permute-start | bytes 786440 | tf_op jit(solution)/shard_map/ppermute | solution.py:30
  266.9 4.3 %collective-permute-start.24 = (f32[512,128]{0,1:T(8,128)S(1)}, f32[512,128]{0,1:T(8,128)S(1)}, u32[]{:S(2)}, u32[]{:S(2)}) collective-permute-start(f32[512,128]{0,1:T(8,128)S(1)} %collective-permute-done.22), channel_id=1, source_target_pairs={{0,15},{1,0},{2,1},{3,2},{4,3},{5,4},{6,5},{7,6},{8,7},{9,8},{10,9... | collective-permute-start | bytes 786440 | tf_op jit(solution)/shard_map/ppermute | solution.py:30
  273.4 4.8 %collective-permute-start.26 = (f32[512,128]{0,1:T(8,128)S(1)}, f32[512,128]{0,1:T(8,128)S(1)}, u32[]{:S(2)}, u32[]{:S(2)}) collective-permute-start(f32[512,128]{0,1:T(8,128)S(1)} %collective-permute-done.24), channel_id=1, source_target_pairs={{0,15},{1,0},{2,1},{3,2},{4,3},{5,4},{6,5},{7,6},{8,7},{9,8},{10,9... | collective-permute-start | bytes 786440 | tf_op jit(solution)/shard_map/ppermute | solution.py:30
  280.5 4.8 %collective-permute-start.28 = (f32[512,128]{0,1:T(8,128)S(1)}, f32[512,128]{0,1:T(8,128)S(1)}, u32[]{:S(2)}, u32[]{:S(2)}) collective-permute-start(f32[512,128]{0,1:T(8,128)S(1)} %collective-permute-done.26), channel_id=1, source_target_pairs={{0,15},{1,0},{2,1},{3,2},{4,3},{5,4},{6,5},{7,6},{8,7},{9,8},{10,9... | collective-permute-start | bytes 786440 | tf_op jit(solution)/shard_map/ppermute | solution.py:30
  288.1 2.0 collective-permute-done.29
  290.8 4.2 %gather_fusion.3 = f32[512,512]{1,0:T(8,128)S(1)} fusion(f32[512,2048]{0,1:T(8,128)} %constant_dynamic-update-slice_fusion, s32[1024]{0:T(1024)S(1)} %pad_clamp_fusion), kind=kCustom, calls=%fused_computation.1.clone | custom fusion | bytes 2099200 | tf_op jit(solution)/shard_map/jit(_take)/gather | solution.py:35
  295.1 1.9 convolution_negate_fusion
  297.0 4.0 %convolution_subtract_fusion = f32[2048,128]{1,0:T(8,128)S(1)} fusion(bf16[512,2048]{1,0:T(8,128)(2,1)} %all-gather.9.cloned.1.call-done, f32[512,128]{1,0:T(8,128)S(1)} %convolution_negate_fusion, bf16[1,2048,128]{2,1,0:T(8,128)(2,1)S(1)} %copy-done.4), kind=kOutput, calls=%fused_computation.10 | convolution fusion | flops 1611137024 | bytes 3932160 | tf_op jit(solution)/shard_map/dot_general | solution.py:45
  301.0 6.3 %fusion.4 = f32[1,2048,128]{1,2,0:T(8,128)S(1)} fusion(f32[2048,128]{1,0:T(8,128)S(1)} %convolution_subtract_fusion, bf16[1,2048,2048]{2,1,0:T(8,128)(2,1)} %all-gather.13.cloned.1.call-done), kind=kOutput, calls=%fused_computation.9 | convolution fusion | flops 6442450944 | bytes 10485760 | tf_op jit(solution)/shard_map/dot_general | solution.py:48
  307.4 1.3 copy.56
  (145 shorter events, 32.1 us)
Async XLA Ops:
  7.2 7.4 %copy-start = (f32[2048,128]{1,0:T(8,128)S(1)}, f32[2048,128]{1,0:T(8,128)}, u32[]{:S(2)}) copy-start(f32[2048,128]{1,0:T(8,128)} %param.12) | copy-start | bytes 3145732
  7.2 11.9 %copy-start.9 = (s32[16,4]{0,1:T(4,128)S(1)}, s32[16,4]{0,1:T(4,128)}, u32[]{:S(2)}) copy-start(s32[16,4]{0,1:T(4,128)} %param.19) | copy-start | bytes 772
  7.2 29.5 %copy-start.10 = (s32[16]{0:T(128)S(1)}, s32[16]{0:T(128)}, u32[]{:S(2)}) copy-start(s32[16]{0:T(128)} %param.21) | copy-start | bytes 196
  7.2 73.0 %all-gather.7.cloned.1.call-start = ((), (), s32[]{:S(2)}) async-start(), calls=%async_computation.1 | async-start | bytes 2228224 | tf_op jit(solution)/shard_map/all_gather | solution.py:42
  9.8 116.1 %all-gather.11.cloned.1.call-start = ((), (), s32[]{:S(2)}) async-start(), calls=%async_computation.3 | async-start | bytes 8912896 | tf_op jit(solution)/shard_map/all_gather | solution.py:49
  10.5 242.8 %all-gather.9.cloned.1.call-start = ((), (), s32[]{:S(2)}) async-start(), calls=%async_computation.2 | async-start | bytes 2228224 | tf_op jit(solution)/shard_map/all_gather | solution.py:42
  13.0 288.0 %all-gather.13.cloned.1.call-start = ((), (), s32[]{:S(2)}) async-start(), calls=%async_computation.4 | async-start | bytes 8912896 | tf_op jit(solution)/shard_map/all_gather | solution.py:49
  15.8 6.4 %collective-permute-start = (f32[512,128]{1,0:T(8,128)S(1)}, f32[512,128]{1,0:T(8,128)S(1)}, u32[]{:S(2)}, u32[]{:S(2)}) collective-permute-start(f32[512,128]{1,0:T(8,128)S(1)} %broadcast_select_fusion), channel_id=1, source_target_pairs={{0,1},{1,2},{2,3},{3,4},{4,5},{5,6},{6,7},{7,8},{8,9},{9,10},{10,1... | collective-permute-start | bytes 786440 | tf_op jit(solution)/shard_map/ppermute | solution.py:27
  18.9 6.1 %collective-permute-start.1 = (f32[512,128]{1,0:T(8,128)S(1)}, f32[512,128]{1,0:T(8,128)S(1)}, u32[]{:S(2)}, u32[]{:S(2)}) collective-permute-start(f32[512,128]{1,0:T(8,128)S(1)} %broadcast_select_fusion), channel_id=1, source_target_pairs={{0,15},{1,0},{2,1},{3,2},{4,3},{5,4},{6,5},{7,6},{8,7},{9,8},{10,9... | collective-permute-start | bytes 786440 | tf_op jit(solution)/shard_map/ppermute | solution.py:30
  22.2 7.2 %collective-permute-start.2 = (f32[512,128]{1,0:T(8,128)S(1)}, f32[512,128]{1,0:T(8,128)S(1)}, u32[]{:S(2)}, u32[]{:S(2)}) collective-permute-start(f32[512,128]{1,0:T(8,128)S(1)} %collective-permute-done), channel_id=1, source_target_pairs={{0,1},{1,2},{2,3},{3,4},{4,5},{5,6},{6,7},{7,8},{8,9},{9,10},{10,1... | collective-permute-start | bytes 786440 | tf_op jit(solution)/shard_map/ppermute | solution.py:27
  25.0 6.9 %collective-permute-start.3 = (f32[512,128]{1,0:T(8,128)S(1)}, f32[512,128]{1,0:T(8,128)S(1)}, u32[]{:S(2)}, u32[]{:S(2)}) collective-permute-start(f32[512,128]{1,0:T(8,128)S(1)} %collective-permute-done.1), channel_id=1, source_target_pairs={{0,15},{1,0},{2,1},{3,2},{4,3},{5,4},{6,5},{7,6},{8,7},{9,8},{10,9... | collective-permute-start | bytes 786440 | tf_op jit(solution)/shard_map/ppermute | solution.py:30
  29.4 10.7 %collective-permute-start.4 = (f32[512,128]{1,0:T(8,128)S(1)}, f32[512,128]{1,0:T(8,128)S(1)}, u32[]{:S(2)}, u32[]{:S(2)}) collective-permute-start(f32[512,128]{1,0:T(8,128)S(1)} %collective-permute-done.2), channel_id=1, source_target_pairs={{0,1},{1,2},{2,3},{3,4},{4,5},{5,6},{6,7},{7,8},{8,9},{9,10},{10,1... | collective-permute-start | bytes 786440 | tf_op jit(solution)/shard_map/ppermute | solution.py:27
  31.9 8.6 %collective-permute-start.5 = (f32[512,128]{1,0:T(8,128)S(1)}, f32[512,128]{1,0:T(8,128)S(1)}, u32[]{:S(2)}, u32[]{:S(2)}) collective-permute-start(f32[512,128]{1,0:T(8,128)S(1)} %collective-permute-done.3), channel_id=1, source_target_pairs={{0,15},{1,0},{2,1},{3,2},{4,3},{5,4},{6,5},{7,6},{8,7},{9,8},{10,9... | collective-permute-start | bytes 786440 | tf_op jit(solution)/shard_map/ppermute | solution.py:30
  40.1 6.5 %collective-permute-start.6 = (f32[512,128]{1,0:T(8,128)S(1)}, f32[512,128]{1,0:T(8,128)S(1)}, u32[]{:S(2)}, u32[]{:S(2)}) collective-permute-start(f32[512,128]{1,0:T(8,128)S(1)} %collective-permute-done.4), channel_id=1, source_target_pairs={{0,1},{1,2},{2,3},{3,4},{4,5},{5,6},{6,7},{7,8},{8,9},{9,10},{10,1... | collective-permute-start | bytes 786440 | tf_op jit(solution)/shard_map/ppermute | solution.py:27
  40.5 7.5 %collective-permute-start.7 = (f32[512,128]{1,0:T(8,128)S(1)}, f32[512,128]{1,0:T(8,128)S(1)}, u32[]{:S(2)}, u32[]{:S(2)}) collective-permute-start(f32[512,128]{1,0:T(8,128)S(1)} %collective-permute-done.5), channel_id=1, source_target_pairs={{0,15},{1,0},{2,1},{3,2},{4,3},{5,4},{6,5},{7,6},{8,7},{9,8},{10,9... | collective-permute-start | bytes 786440 | tf_op jit(solution)/shard_map/ppermute | solution.py:30
  46.6 8.4 %collective-permute-start.8 = (f32[512,128]{1,0:T(8,128)S(1)}, f32[512,128]{1,0:T(8,128)S(1)}, u32[]{:S(2)}, u32[]{:S(2)}) collective-permute-start(f32[512,128]{1,0:T(8,128)S(1)} %collective-permute-done.6), channel_id=1, source_target_pairs={{0,1},{1,2},{2,3},{3,4},{4,5},{5,6},{6,7},{7,8},{8,9},{9,10},{10,1... | collective-permute-start | bytes 786440 | tf_op jit(solution)/shard_map/ppermute | solution.py:27
  48.0 7.8 %collective-permute-start.9 = (f32[512,128]{1,0:T(8,128)S(1)}, f32[512,128]{1,0:T(8,128)S(1)}, u32[]{:S(2)}, u32[]{:S(2)}) collective-permute-start(f32[512,128]{1,0:T(8,128)S(1)} %collective-permute-done.7), channel_id=1, source_target_pairs={{0,15},{1,0},{2,1},{3,2},{4,3},{5,4},{6,5},{7,6},{8,7},{9,8},{10,9... | collective-permute-start | bytes 786440 | tf_op jit(solution)/shard_map/ppermute | solution.py:30
  55.0 7.0 %collective-permute-start.10 = (f32[512,128]{1,0:T(8,128)S(1)}, f32[512,128]{1,0:T(8,128)S(1)}, u32[]{:S(2)}, u32[]{:S(2)}) collective-permute-start(f32[512,128]{1,0:T(8,128)S(1)} %collective-permute-done.8), channel_id=1, source_target_pairs={{0,1},{1,2},{2,3},{3,4},{4,5},{5,6},{6,7},{7,8},{8,9},{9,10},{10,1... | collective-permute-start | bytes 786440 | tf_op jit(solution)/shard_map/ppermute | solution.py:27
  55.9 7.0 %collective-permute-start.11 = (f32[512,128]{1,0:T(8,128)S(1)}, f32[512,128]{1,0:T(8,128)S(1)}, u32[]{:S(2)}, u32[]{:S(2)}) collective-permute-start(f32[512,128]{1,0:T(8,128)S(1)} %collective-permute-done.9), channel_id=1, source_target_pairs={{0,15},{1,0},{2,1},{3,2},{4,3},{5,4},{6,5},{7,6},{8,7},{9,8},{10,9... | collective-permute-start | bytes 786440 | tf_op jit(solution)/shard_map/ppermute | solution.py:30
  62.1 7.0 %collective-permute-start.12 = (f32[512,128]{1,0:T(8,128)S(1)}, f32[512,128]{1,0:T(8,128)S(1)}, u32[]{:S(2)}, u32[]{:S(2)}) collective-permute-start(f32[512,128]{1,0:T(8,128)S(1)} %collective-permute-done.10), channel_id=1, source_target_pairs={{0,1},{1,2},{2,3},{3,4},{4,5},{5,6},{6,7},{7,8},{8,9},{9,10},{10,1... | collective-permute-start | bytes 786440 | tf_op jit(solution)/shard_map/ppermute | solution.py:27
  62.9 7.0 %collective-permute-start.13 = (f32[512,128]{1,0:T(8,128)S(1)}, f32[512,128]{1,0:T(8,128)S(1)}, u32[]{:S(2)}, u32[]{:S(2)}) collective-permute-start(f32[512,128]{1,0:T(8,128)S(1)} %collective-permute-done.11), channel_id=1, source_target_pairs={{0,15},{1,0},{2,1},{3,2},{4,3},{5,4},{6,5},{7,6},{8,7},{9,8},{10,9... | collective-permute-start | bytes 786440 | tf_op jit(solution)/shard_map/ppermute | solution.py:30
  69.0 6.0 %collective-permute-start.14 = (f32[512,128]{1,0:T(8,128)S(1)}, f32[512,128]{1,0:T(8,128)S(1)}, u32[]{:S(2)}, u32[]{:S(2)}) collective-permute-start(f32[512,128]{1,0:T(8,128)S(1)} %collective-permute-done.12), channel_id=1, source_target_pairs={{0,1},{1,2},{2,3},{3,4},{4,5},{5,6},{6,7},{7,8},{8,9},{9,10},{10,1... | collective-permute-start | bytes 786440 | tf_op jit(solution)/shard_map/ppermute | solution.py:27
  75.9 4.3 %copy-start.3 = (bf16[1,2048,128]{2,1,0:T(8,128)(2,1)S(1)}, bf16[1,2048,128]{2,1,0:T(8,128)(2,1)}, u32[]{:S(2)}) copy-start(bf16[1,2048,128]{2,1,0:T(8,128)(2,1)} %param.13) | copy-start | bytes 1572868
  80.2 4.4 %copy-start.2 = (bf16[512,2048]{1,0:T(8,128)(2,1)S(1)}, bf16[512,2048]{1,0:T(8,128)(2,1)}, u32[]{:S(2)}) copy-start(bf16[512,2048]{1,0:T(8,128)(2,1)} %all-gather.7.cloned.1.call-done) | copy-start | bytes 6291460
  84.6 47.6 %copy-start.5 = (f32[512,128]{1,0:T(8,128)}, f32[512,128]{1,0:T(8,128)S(1)}, u32[]{:S(2)}) copy-start(f32[512,128]{1,0:T(8,128)S(1)} %convolution_negate_fusion.1) | copy-start | bytes 786436
  165.5 69.8 %all-to-all-start = ((f32[16,512,128]{2,1,0:T(8,128)}), f32[16,512,128]{2,1,0:T(8,128)}, u32[]{:S(2)}, u32[]{:S(2)}) async-start(f32[16,512,128]{2,1,0:T(8,128)} %select_multiply_fusion), calls=%async_computation | async-start | bytes 8388608 | tf_op jit(solution)/shard_map/all_to_all | solution.py:82
  172.5 80.9 %copy-start.4 = (bf16[1,2048,128]{2,1,0:T(8,128)(2,1)S(1)}, bf16[1,2048,128]{2,1,0:T(8,128)(2,1)}, u32[]{:S(2)}) copy-start(bf16[1,2048,128]{2,1,0:T(8,128)(2,1)} %param.17) | copy-start | bytes 1572868
  237.9 4.5 %collective-permute-start.15 = (f32[512,128]{0,1:T(8,128)S(1)}, f32[512,128]{0,1:T(8,128)S(1)}, u32[]{:S(2)}, u32[]{:S(2)}) collective-permute-start(f32[512,128]{0,1:T(8,128)S(1)} %copy.52), channel_id=1, source_target_pairs={{0,1},{1,2},{2,3},{3,4},{4,5},{5,6},{6,7},{7,8},{8,9},{9,10},{10,1... | collective-permute-start | bytes 786440 | tf_op jit(solution)/shard_map/ppermute | solution.py:27
  239.1 6.1 %collective-permute-start.16 = (f32[512,128]{0,1:T(8,128)S(1)}, f32[512,128]{0,1:T(8,128)S(1)}, u32[]{:S(2)}, u32[]{:S(2)}) collective-permute-start(f32[512,128]{0,1:T(8,128)S(1)} %copy.52), channel_id=1, source_target_pairs={{0,15},{1,0},{2,1},{3,2},{4,3},{5,4},{6,5},{7,6},{8,7},{9,8},{10,9... | collective-permute-start | bytes 786440 | tf_op jit(solution)/shard_map/ppermute | solution.py:30
  242.5 10.9 %copy-start.7 = (f32[512,128]{0,1:T(8,128)}, f32[512,128]{0,1:T(8,128)S(1)}, u32[]{:S(2)}) copy-start(f32[512,128]{0,1:T(8,128)S(1)} %collective-permute-done.15) | copy-start | bytes 786436
  242.5 5.8 %collective-permute-start.17 = (f32[512,128]{0,1:T(8,128)S(1)}, f32[512,128]{0,1:T(8,128)S(1)}, u32[]{:S(2)}, u32[]{:S(2)}) collective-permute-start(f32[512,128]{0,1:T(8,128)S(1)} %collective-permute-done.15), channel_id=1, source_target_pairs={{0,1},{1,2},{2,3},{3,4},{4,5},{5,6},{6,7},{7,8},{8,9},{9,10},{10,1... | collective-permute-start | bytes 786440 | tf_op jit(solution)/shard_map/ppermute | solution.py:27
  245.2 6.1 %collective-permute-start.18 = (f32[512,128]{0,1:T(8,128)S(1)}, f32[512,128]{0,1:T(8,128)S(1)}, u32[]{:S(2)}, u32[]{:S(2)}) collective-permute-start(f32[512,128]{0,1:T(8,128)S(1)} %collective-permute-done.16), channel_id=1, source_target_pairs={{0,15},{1,0},{2,1},{3,2},{4,3},{5,4},{6,5},{7,6},{8,7},{9,8},{10,9... | collective-permute-start | bytes 786440 | tf_op jit(solution)/shard_map/ppermute | solution.py:30
  248.3 8.7 %collective-permute-start.19 = (f32[512,128]{0,1:T(8,128)S(1)}, f32[512,128]{0,1:T(8,128)S(1)}, u32[]{:S(2)}, u32[]{:S(2)}) collective-permute-start(f32[512,128]{0,1:T(8,128)S(1)} %collective-permute-done.17), channel_id=1, source_target_pairs={{0,1},{1,2},{2,3},{3,4},{4,5},{5,6},{6,7},{7,8},{8,9},{9,10},{10,1... | collective-permute-start | bytes 786440 | tf_op jit(solution)/shard_map/ppermute | solution.py:27
  251.3 9.7 %collective-permute-start.20 = (f32[512,128]{0,1:T(8,128)S(1)}, f32[512,128]{0,1:T(8,128)S(1)}, u32[]{:S(2)}, u32[]{:S(2)}) collective-permute-start(f32[512,128]{0,1:T(8,128)S(1)} %collective-permute-done.18), channel_id=1, source_target_pairs={{0,15},{1,0},{2,1},{3,2},{4,3},{5,4},{6,5},{7,6},{8,7},{9,8},{10,9... | collective-permute-start | bytes 786440 | tf_op jit(solution)/shard_map/ppermute | solution.py:30
  256.9 3.3 %copy-start.8 = (f32[512,128]{0,1:T(8,128)S(1)}, f32[512,128]{0,1:T(8,128)}, u32[]{:S(2)}) copy-start(f32[512,128]{0,1:T(8,128)} %copy-done.7) | copy-start | bytes 786436
  257.0 8.2 %collective-permute-start.21 = (f32[512,128]{0,1:T(8,128)S(1)}, f32[512,128]{0,1:T(8,128)S(1)}, u32[]{:S(2)}, u32[]{:S(2)}) collective-permute-start(f32[512,128]{0,1:T(8,128)S(1)} %collective-permute-done.19), channel_id=1, source_target_pairs={{0,1},{1,2},{2,3},{3,4},{4,5},{5,6},{6,7},{7,8},{8,9},{9,10},{10,1... | collective-permute-start | bytes 786440 | tf_op jit(solution)/shard_map/ppermute | solution.py:27
  261.0 5.9 %collective-permute-start.22 = (f32[512,128]{0,1:T(8,128)S(1)}, f32[512,128]{0,1:T(8,128)S(1)}, u32[]{:S(2)}, u32[]{:S(2)}) collective-permute-start(f32[512,128]{0,1:T(8,128)S(1)} %collective-permute-done.20), channel_id=1, source_target_pairs={{0,15},{1,0},{2,1},{3,2},{4,3},{5,4},{6,5},{7,6},{8,7},{9,8},{10,9... | collective-permute-start | bytes 786440 | tf_op jit(solution)/shard_map/ppermute | solution.py:30
  265.1 6.9 %collective-permute-start.23 = (f32[512,128]{0,1:T(8,128)S(1)}, f32[512,128]{0,1:T(8,128)S(1)}, u32[]{:S(2)}, u32[]{:S(2)}) collective-permute-start(f32[512,128]{0,1:T(8,128)S(1)} %collective-permute-done.21), channel_id=1, source_target_pairs={{0,1},{1,2},{2,3},{3,4},{4,5},{5,6},{6,7},{7,8},{8,9},{9,10},{10,1... | collective-permute-start | bytes 786440 | tf_op jit(solution)/shard_map/ppermute | solution.py:27
  266.9 6.5 %collective-permute-start.24 = (f32[512,128]{0,1:T(8,128)S(1)}, f32[512,128]{0,1:T(8,128)S(1)}, u32[]{:S(2)}, u32[]{:S(2)}) collective-permute-start(f32[512,128]{0,1:T(8,128)S(1)} %collective-permute-done.22), channel_id=1, source_target_pairs={{0,15},{1,0},{2,1},{3,2},{4,3},{5,4},{6,5},{7,6},{8,7},{9,8},{10,9... | collective-permute-start | bytes 786440 | tf_op jit(solution)/shard_map/ppermute | solution.py:30
  272.0 7.0 %collective-permute-start.25 = (f32[512,128]{0,1:T(8,128)S(1)}, f32[512,128]{0,1:T(8,128)S(1)}, u32[]{:S(2)}, u32[]{:S(2)}) collective-permute-start(f32[512,128]{0,1:T(8,128)S(1)} %collective-permute-done.23), channel_id=1, source_target_pairs={{0,1},{1,2},{2,3},{3,4},{4,5},{5,6},{6,7},{7,8},{8,9},{9,10},{10,1... | collective-permute-start | bytes 786440 | tf_op jit(solution)/shard_map/ppermute | solution.py:27
  273.4 7.0 %collective-permute-start.26 = (f32[512,128]{0,1:T(8,128)S(1)}, f32[512,128]{0,1:T(8,128)S(1)}, u32[]{:S(2)}, u32[]{:S(2)}) collective-permute-start(f32[512,128]{0,1:T(8,128)S(1)} %collective-permute-done.24), channel_id=1, source_target_pairs={{0,15},{1,0},{2,1},{3,2},{4,3},{5,4},{6,5},{7,6},{8,7},{9,8},{10,9... | collective-permute-start | bytes 786440 | tf_op jit(solution)/shard_map/ppermute | solution.py:30
  279.0 7.0 %collective-permute-start.27 = (f32[512,128]{0,1:T(8,128)S(1)}, f32[512,128]{0,1:T(8,128)S(1)}, u32[]{:S(2)}, u32[]{:S(2)}) collective-permute-start(f32[512,128]{0,1:T(8,128)S(1)} %collective-permute-done.25), channel_id=1, source_target_pairs={{0,1},{1,2},{2,3},{3,4},{4,5},{5,6},{6,7},{7,8},{8,9},{9,10},{10,1... | collective-permute-start | bytes 786440 | tf_op jit(solution)/shard_map/ppermute | solution.py:27
  280.5 7.0 %collective-permute-start.28 = (f32[512,128]{0,1:T(8,128)S(1)}, f32[512,128]{0,1:T(8,128)S(1)}, u32[]{:S(2)}, u32[]{:S(2)}) collective-permute-start(f32[512,128]{0,1:T(8,128)S(1)} %collective-permute-done.26), channel_id=1, source_target_pairs={{0,15},{1,0},{2,1},{3,2},{4,3},{5,4},{6,5},{7,6},{8,7},{9,8},{10,9... | collective-permute-start | bytes 786440 | tf_op jit(solution)/shard_map/ppermute | solution.py:30
  286.0 4.2 %collective-permute-start.29 = (f32[512,128]{0,1:T(8,128)S(1)}, f32[512,128]{0,1:T(8,128)S(1)}, u32[]{:S(2)}, u32[]{:S(2)}) collective-permute-start(f32[512,128]{0,1:T(8,128)S(1)} %collective-permute-done.27), channel_id=1, source_target_pairs={{0,1},{1,2},{2,3},{3,4},{4,5},{5,6},{6,7},{7,8},{8,9},{9,10},{10,1... | collective-permute-start | bytes 786440 | tf_op jit(solution)/shard_map/ppermute | solution.py:27
  297.0 10.4 %copy-start.6 = (f32[512,128]{1,0:T(8,128)}, f32[512,128]{1,0:T(8,128)S(1)}, u32[]{:S(2)}) copy-start(f32[512,128]{1,0:T(8,128)S(1)} %convolution_negate_fusion) | copy-start | bytes 786436
  301.0 7.7 %copy-start.1 = (f32[2048,128]{1,0:T(8,128)S(1)}, f32[2048,128]{1,0:T(8,128)}, u32[]{:S(2)}) copy-start(f32[2048,128]{1,0:T(8,128)} %param.12) | copy-start | bytes 3145732
Sparse Core Ops, SparseCore 0:
  10.4 49.2 all-gather.6
  61.4 64.4 all-gather.10
  128.2 39.5 all-gather.8
  169.4 64.3 all-gather.12
